TPU v7x, 32 devices: a whole 2x2x4 slice. The times are simulated.
32 devices in a mesh: ctx: 8 (over z, core), dp: 2 (over x), ws: 2 (over y).
Axes of the slice: x: 2, y: 2, z: 4, core: 2. Of those that a mesh axis runs over, the one named last changes fastest.
Arguments:
- byte_ids: int32 [4, 8064], P(('dp', 'ws'), 'ctx'), may hold values from 0 to 258
- segments: int32 [4, 8064], P(('dp', 'ws'), 'ctx'), may hold values from 0 to 15, as said below
- embed: bfloat16 [259, 768], P(None, 'ws'), may hold values from -6 to 6
- conv_kernel: bfloat16 [5, 768], replicated, may hold values from -2.6875 to 2.6875
- score_weight: bfloat16 [768], replicated, may hold values from -0.21875 to 0.21875
- attn_gain: float32 [768], replicated, may hold values from 0.5 to 1.5
- w_q: bfloat16 [768, 768], P('ws'), may hold values from -0.0546875 to 0.0546875
- w_k: bfloat16 [768, 768], P('ws'), may hold values from -0.21875 to 0.21875
- w_v: bfloat16 [768, 768], P('ws'), may hold values from -0.21875 to 0.21875
- w_o: bfloat16 [768, 768], P('ws'), may hold values from -0.625 to 0.625
- rel_bias: float32 [32, 12], replicated, may hold values from -4 to 4
- ff_gain: float32 [768], replicated, may hold values from 0.5 to 1.5
- w_gate: bfloat16 [768, 2048], P('ws'), may hold values from -0.21875 to 0.21875
- w_up: bfloat16 [768, 2048], P('ws'), may hold values from -0.21875 to 0.21875
- w_down: bfloat16 [2048, 768], P('ws'), may hold values from -0.125 to 0.125
- cotangent: bfloat16 [4, 4032, 768], P(('dp', 'ws'), 'ctx'), may hold values from -6 to 6
Outputs:
- output: bfloat16 [4, 4032, 768], P(('dp', 'ws'), 'ctx')
- byte_grad: float32 [4, 8064, 768], P(('dp', 'ws'), 'ctx')
- embed_grad: float32 [259, 768], P(None, 'ws')
- conv_grad: float32 [5, 768], replicated
- score_grad: float32 [768], replicated
- attn_gain_grad: float32 [768], replicated
- q_grad: float32 [768, 768], P('ws')
- k_grad: float32 [768, 768], P('ws')
- v_grad: float32 [768, 768], P('ws')
- o_grad: float32 [768, 768], P('ws')
- bias_grad: float32 [32, 12], replicated
- ff_gain_grad: float32 [768], replicated
- gate_grad: float32 [768, 2048], P('ws')
- up_grad: float32 [768, 2048], P('ws')
- down_grad: float32 [2048, 768], P('ws')
Inputs may be any that keep to these rules, and one draw needn't show every extreme that they name: `segments`: in each sequence the document numbers start at 0 and rise by one at each document's first byte; documents begin at multiples of 4 bytes and hold 124 to 1008 bytes, except the last one, which the sequence's end may cut short; some document of each sequence holds exactly 1008 bytes; every sequence has the same number of documents.
All inputs are finite; a program needn't handle non-finite values.
Results may differ from a plain program's by a relative error of at most 0.02.
Values may be sent and summed in bfloat16 or wider, within the bound.
No kernel may reach another device: no remote copies, remote signals or barrier semaphores. Data moves between devices by JAX's collectives and lax.ppermute only.
A program may use at most 192 MiB of HBM per device.

v0:
```python
import jax
import jax.numpy as jnp
from jax import lax
from jax.sharding import PartitionSpec as P

thresholds = (12, 16, 23, 32, 46, 64, 91)
negative = -1e30
epsilon = 1e-06
highest = lax.Precision.HIGHEST


def extended(block, sides, width):
    for axis, dim in sides:
        count = lax.axis_size(axis)
        forward = [(i, i + 1) for i in range(count - 1)]
        backward = [(target, source) for source, target in forward]
        low = lax.ppermute(
            lax.slice_in_dim(block, block.shape[dim] - width, None, axis=dim), axis, forward
        )
        high = lax.ppermute(lax.slice_in_dim(block, 0, width, axis=dim), axis, backward)
        block = jnp.concatenate([low, block, high], axis=dim)
    return block


def bucket_of(relative):
    distance = jnp.abs(relative)
    far_bucket = 8 + sum(((distance >= threshold).astype(jnp.int32) for threshold in thresholds))
    near_bucket = jnp.where(distance < 8, distance, far_bucket)
    return near_bucket + 16 * (relative > 0).astype(jnp.int32)


def contract(left_side, right_side, left_axis, right_axis):
    return lax.dot_general(
        left_side,
        right_side,
        (((left_axis,), (right_axis,)), ((), ())),
        preferred_element_type=jnp.float32,
    )


def inverse_rms(values):
    return lax.rsqrt(jnp.mean(values * values, axis=-1, keepdims=True) + epsilon)


def pool_blocks(conv_out):
    byte_count, channels = conv_out.shape
    pooled = []
    for block_size in (1, 2, 3, 4):
        block_means = jnp.mean(
            conv_out.reshape(byte_count // block_size, block_size, channels), axis=1
        )
        pooled.append(jnp.repeat(block_means, block_size, axis=0))
    return pooled


def unpool_blocks(grad_list):
    byte_count, channels = grad_list[0].shape
    summed = jnp.zeros((byte_count, channels), jnp.float32)
    for block_size, grad_part in zip((1, 2, 3, 4), grad_list):
        block_sums = (
            jnp.sum(grad_part.reshape(byte_count // block_size, block_size, channels), axis=1)
            / block_size
        )
        summed = summed + jnp.repeat(block_sums, block_size, axis=0)
    return summed


def diagonal_sums(score_grid):
    row_total, col_total = score_grid.shape
    wider_grid = jnp.pad(score_grid, ((0, 0), (0, row_total)))
    flat_grid = jnp.pad(wider_grid.reshape(-1), (0, row_total))
    skewed = flat_grid.reshape(row_total, col_total + row_total + 1)
    return jnp.sum(skewed[:, :col_total], axis=0)


def head_slice(matrix, head_number, head_dim):
    return lax.dynamic_slice_in_dim(matrix, head_number * head_dim, head_dim, 1)


def merge_heads(per_head):
    return jnp.transpose(per_head, (1, 0, 2)).reshape(per_head.shape[1], -1)


def head_scores(query_part, key_part, bias_column, bucket, allowed):
    raw_scores = contract(query_part, key_part, 1, 1)
    return jnp.where(allowed, raw_scores + jnp.take(bias_column, bucket), negative)


def per_device(
    byte_ids,
    segments,
    embed,
    conv_kernel,
    score_weight,
    attn_gain,
    w_q,
    w_k,
    w_v,
    w_o,
    rel_bias,
    ff_gain,
    w_gate,
    w_up,
    w_down,
    cotangent,
):
    byte_count = byte_ids.shape[1]
    row_count = byte_count // 2
    cycle_count = lax.axis_size("ctx")
    cycle_place = lax.axis_index("ctx")
    head_count = rel_bias.shape[1]
    bucket_count = rel_bias.shape[0]
    kernel_width = conv_kernel.shape[0]
    half_width = (kernel_width - 1) // 2
    id_stack = jnp.stack([byte_ids[0], segments[0]])
    id_rim = extended(id_stack, (("ctx", 1),), byte_count)
    byte_place = (cycle_place - 1) * byte_count + jnp.arange(3 * byte_count, dtype=jnp.int32)
    byte_valid = (byte_place >= 0) & (byte_place < cycle_count * byte_count)
    gathered = (
        lax.all_gather(embed, "ws", axis=1, tiled=True),
        lax.all_gather(w_q, "ws", axis=0, tiled=True),
        lax.all_gather(w_k, "ws", axis=0, tiled=True),
        lax.all_gather(w_v, "ws", axis=0, tiled=True),
        lax.all_gather(w_o, "ws", axis=0, tiled=True),
        lax.all_gather(w_gate, "ws", axis=0, tiled=True),
        lax.all_gather(w_up, "ws", axis=0, tiled=True),
        lax.all_gather(w_down, "ws", axis=0, tiled=True),
    )
    embed_table, query_w, key_w, value_w, out_w, gate_w, up_w, down_w = gathered
    lookup_ids = id_rim[0, byte_count - half_width : 2 * byte_count + half_width]
    lookup_valid = byte_valid[byte_count - half_width : 2 * byte_count + half_width]
    vocab_range = jnp.arange(embed_table.shape[0], dtype=jnp.int32)
    one_hot = ((lookup_ids[:, None] == vocab_range[None, :]) & lookup_valid[:, None]).astype(
        jnp.bfloat16
    )
    embedded = jnp.dot(one_hot, embed_table, preferred_element_type=jnp.float32)
    kernel = conv_kernel.astype(jnp.float32)
    conv_out = kernel[0] * embedded[0:byte_count]
    for offset in range(1, kernel_width):
        conv_out = conv_out + kernel[offset] * embedded[offset : offset + byte_count]
    pooled = pool_blocks(conv_out)
    score_vec = score_weight.astype(jnp.float32)
    block_scores = jnp.stack(
        [jnp.dot(pooled_part, score_vec, precision=highest) for pooled_part in pooled], axis=1
    )
    block_weight = jax.nn.softmax(block_scores, axis=1)
    latent = block_weight[:, 0:1] * pooled[0]
    for number in range(1, 4):
        latent = latent + block_weight[:, number : number + 1] * pooled[number]
    start_rows = jnp.mean(latent.reshape(row_count, 2, -1), axis=1)
    inverse_one = inverse_rms(start_rows)
    normed_one = start_rows * inverse_one
    first_in = (normed_one * attn_gain).astype(jnp.bfloat16)
    queries = jnp.dot(first_in, query_w, preferred_element_type=jnp.float32).astype(jnp.bfloat16)
    keys_own = jnp.dot(first_in, key_w, preferred_element_type=jnp.float32).astype(jnp.bfloat16)
    values_own = jnp.dot(first_in, value_w, preferred_element_type=jnp.float32).astype(jnp.bfloat16)
    key_value = extended(jnp.stack([keys_own, values_own]), (("ctx", 1),), row_count)
    row_segs = id_rim[1, ::2]
    row_valid = byte_valid[::2]
    own_segs = row_segs[row_count : 2 * row_count]
    wide_range = jnp.arange(3 * row_count, dtype=jnp.int32)
    own_range = jnp.arange(row_count, dtype=jnp.int32)
    allowed = (own_segs[:, None] == row_segs[None, :]) & row_valid[None, :]
    bucket = bucket_of(wide_range[None, :] - row_count - own_range[:, None])
    head_dim = queries.shape[1] // head_count
    head_range = jnp.arange(head_count, dtype=jnp.int32)

    def forward_head(head_number):
        query_part = head_slice(queries, head_number, head_dim)
        key_part = head_slice(key_value[0], head_number, head_dim)
        value_part = head_slice(key_value[1], head_number, head_dim)
        bias_column = lax.dynamic_slice_in_dim(rel_bias, head_number, 1, 1)[:, 0]
        scores = head_scores(query_part, key_part, bias_column, bucket, allowed)
        row_max = jnp.max(scores, axis=1, keepdims=True)
        exponent = jnp.exp(scores - row_max)
        denominator = jnp.sum(exponent, axis=1, keepdims=True)
        attn_probs = (exponent / denominator).astype(jnp.bfloat16)
        head_mix = jnp.dot(attn_probs, value_part, preferred_element_type=jnp.float32)
        return (head_mix, (row_max + jnp.log(denominator))[:, 0])

    head_out, log_norm = lax.map(forward_head, head_range)
    attended = merge_heads(head_out).astype(jnp.bfloat16)
    middle = start_rows + jnp.dot(attended, out_w, preferred_element_type=jnp.float32)
    inverse_two = inverse_rms(middle)
    normed_two = middle * inverse_two
    second_in = (normed_two * ff_gain).astype(jnp.bfloat16)
    gate_pre = jnp.dot(second_in, gate_w, preferred_element_type=jnp.float32)
    up_pre = jnp.dot(second_in, up_w, preferred_element_type=jnp.float32)
    gelu_gate, gelu_pull = jax.vjp(
        lambda pre_values: jax.nn.gelu(pre_values, approximate=True), gate_pre
    )
    hidden = (gelu_gate * up_pre).astype(jnp.bfloat16)
    output = (middle + jnp.dot(hidden, down_w, preferred_element_type=jnp.float32)).astype(
        jnp.bfloat16
    )
    back_weights = (
        lax.all_gather(w_q, "ws", axis=0, tiled=True),
        lax.all_gather(w_k, "ws", axis=0, tiled=True),
        lax.all_gather(w_v, "ws", axis=0, tiled=True),
        lax.all_gather(w_o, "ws", axis=0, tiled=True),
        lax.all_gather(w_gate, "ws", axis=0, tiled=True),
        lax.all_gather(w_up, "ws", axis=0, tiled=True),
        lax.all_gather(w_down, "ws", axis=0, tiled=True),
    )
    query_w, key_w, value_w, out_w, gate_w, up_w, down_w = back_weights
    grad_low = cotangent[0]
    grad_out = grad_low.astype(jnp.float32)
    down_grad = contract(hidden, grad_low, 0, 0)
    d_hidden = contract(grad_low, down_w, 1, 1)
    d_gate = gelu_pull(d_hidden * up_pre)[0].astype(jnp.bfloat16)
    d_up = (d_hidden * gelu_gate).astype(jnp.bfloat16)
    gate_grad = contract(second_in, d_gate, 0, 0)
    up_grad = contract(second_in, d_up, 0, 0)
    d_second = contract(d_gate, gate_w, 1, 1) + contract(d_up, up_w, 1, 1)
    ff_gain_grad = jnp.sum(d_second * normed_two, axis=0)
    d_normed_two = d_second * ff_gain
    d_middle = grad_out + inverse_two * (
        d_normed_two - normed_two * jnp.mean(d_normed_two * normed_two, axis=-1, keepdims=True)
    )
    d_branch = d_middle.astype(jnp.bfloat16)
    out_grad = contract(attended, d_branch, 0, 0)
    d_attended = contract(d_branch, out_w, 1, 1).astype(jnp.bfloat16)
    line_onehot = (
        bucket_of(wide_range - row_count)[:, None]
        == jnp.arange(bucket_count, dtype=jnp.int32)[None, :]
    ).astype(jnp.float32)

    def score_grads(head_number):
        query_part = head_slice(queries, head_number, head_dim)
        key_part = head_slice(key_value[0], head_number, head_dim)
        value_part = head_slice(key_value[1], head_number, head_dim)
        grad_part = head_slice(d_attended, head_number, head_dim)
        bias_column = lax.dynamic_slice_in_dim(rel_bias, head_number, 1, 1)[:, 0]
        scores = head_scores(query_part, key_part, bias_column, bucket, allowed)
        attn_weights = jnp.exp(scores - log_norm[head_number][:, None])
        d_prob = contract(grad_part, value_part, 1, 1)
        delta_row = jnp.sum(attn_weights * d_prob, axis=1)
        d_score = attn_weights * (d_prob - delta_row[:, None])
        bias_part = jnp.dot(diagonal_sums(d_score), line_onehot, precision=highest)
        d_score_low = d_score.astype(jnp.bfloat16)
        d_query = jnp.dot(d_score_low, key_part, preferred_element_type=jnp.float32)
        return (attn_weights, d_score_low, d_query, delta_row, bias_part, query_part, grad_part)

    def query_head(head_number):
        attn_weights, d_score_low, d_query, delta_row, bias_part, query_part, grad_part = (
            score_grads(head_number)
        )
        return (d_query, bias_part, delta_row)

    d_query_heads, bias_heads, delta_heads = lax.map(query_head, head_range)
    query_rim = extended(jnp.stack([queries, d_attended]), (("ctx", 1),), row_count)
    stat_rim = extended(jnp.stack([log_norm, delta_heads]), (("ctx", 2),), row_count)
    allowed_back = (row_segs[:, None] == own_segs[None, :]) & row_valid[:, None]
    bucket_back = bucket_of(own_range[None, :] - wide_range[:, None] + row_count)

    def key_head(head_number):
        query_part = head_slice(query_rim[0], head_number, head_dim)
        grad_part = head_slice(query_rim[1], head_number, head_dim)
        key_part = head_slice(keys_own, head_number, head_dim)
        value_part = head_slice(values_own, head_number, head_dim)
        bias_column = lax.dynamic_slice_in_dim(rel_bias, head_number, 1, 1)[:, 0]
        scores = head_scores(query_part, key_part, bias_column, bucket_back, allowed_back)
        attn_weights = jnp.exp(scores - stat_rim[0, head_number][:, None])
        d_prob = contract(grad_part, value_part, 1, 1)
        d_score = attn_weights * (d_prob - stat_rim[1, head_number][:, None])
        d_key = contract(d_score.astype(jnp.bfloat16), query_part, 0, 0)
        d_value = contract(attn_weights.astype(jnp.bfloat16), grad_part, 0, 0)
        return (d_key, d_value)

    d_key_heads, d_value_heads = lax.map(key_head, head_range)
    own_grads = jnp.stack([merge_heads(d_key_heads), merge_heads(d_value_heads)])
    d_queries = merge_heads(d_query_heads).astype(jnp.bfloat16)
    d_keys = own_grads[0].astype(jnp.bfloat16)
    d_values = own_grads[1].astype(jnp.bfloat16)
    bias_grad = jnp.transpose(bias_heads)
    q_grad = contract(first_in, d_queries, 0, 0)
    k_grad = contract(first_in, d_keys, 0, 0)
    v_grad = contract(first_in, d_values, 0, 0)
    d_first = (
        contract(d_queries, query_w, 1, 1)
        + contract(d_keys, key_w, 1, 1)
        + contract(d_values, value_w, 1, 1)
    )
    attn_gain_grad = jnp.sum(d_first * normed_one, axis=0)
    d_normed_one = d_first * attn_gain
    d_start = d_middle + inverse_one * (
        d_normed_one - normed_one * jnp.mean(d_normed_one * normed_one, axis=-1, keepdims=True)
    )
    d_latent = jnp.repeat(d_start * 0.5, 2, axis=0)
    d_block = jnp.stack([jnp.sum(d_latent * pooled_part, axis=1) for pooled_part in pooled], axis=1)
    d_block_scores = block_weight * (
        d_block - jnp.sum(block_weight * d_block, axis=1, keepdims=True)
    )
    score_grad = jnp.dot(d_block_scores[:, 0], pooled[0], precision=highest)
    for number in range(1, 4):
        score_grad = score_grad + jnp.dot(
            d_block_scores[:, number], pooled[number], precision=highest
        )
    d_pooled = [
        block_weight[:, number : number + 1] * d_latent
        + d_block_scores[:, number : number + 1] * score_vec[None, :]
        for number in range(4)
    ]
    d_conv = unpool_blocks(d_pooled)
    conv_rim = extended(d_conv.astype(jnp.bfloat16), (("ctx", 0),), half_width).astype(d_conv.dtype)
    conv_grad = jnp.stack(
        [
            jnp.sum(d_conv * embedded[offset : offset + byte_count], axis=0)
            for offset in range(kernel_width)
        ]
    )
    byte_grad = kernel[0] * conv_rim[2 * half_width : 2 * half_width + byte_count]
    for offset in range(1, kernel_width):
        byte_grad = (
            byte_grad
            + kernel[offset]
            * conv_rim[2 * half_width - offset : 2 * half_width - offset + byte_count]
        )
    own_hot = one_hot[half_width : half_width + byte_count].astype(jnp.float32)
    embed_full = lax.dot_general(
        own_hot,
        byte_grad,
        (((0,), (0,)), ((), ())),
        precision=highest,
        preferred_element_type=jnp.float32,
    )
    large_sums = (
        lax.psum_scatter(
            embed_full.astype(jnp.bfloat16), "ws", scatter_dimension=1, tiled=True
        ).astype(jnp.float32),
        lax.psum_scatter(q_grad.astype(jnp.bfloat16), "ws", scatter_dimension=0, tiled=True).astype(
            jnp.float32
        ),
        lax.psum_scatter(k_grad.astype(jnp.bfloat16), "ws", scatter_dimension=0, tiled=True).astype(
            jnp.float32
        ),
        lax.psum_scatter(v_grad.astype(jnp.bfloat16), "ws", scatter_dimension=0, tiled=True).astype(
            jnp.float32
        ),
        lax.psum_scatter(
            out_grad.astype(jnp.bfloat16), "ws", scatter_dimension=0, tiled=True
        ).astype(jnp.float32),
        lax.psum_scatter(
            gate_grad.astype(jnp.bfloat16), "ws", scatter_dimension=0, tiled=True
        ).astype(jnp.float32),
        lax.psum_scatter(
            up_grad.astype(jnp.bfloat16), "ws", scatter_dimension=0, tiled=True
        ).astype(jnp.float32),
        lax.psum_scatter(
            down_grad.astype(jnp.bfloat16), "ws", scatter_dimension=0, tiled=True
        ).astype(jnp.float32),
    )
    large_sums = (
        lax.psum(large_sums[0].astype(jnp.bfloat16), ("ctx", "dp")).astype(jnp.float32),
        lax.psum(large_sums[1].astype(jnp.bfloat16), ("ctx", "dp")).astype(jnp.float32),
        lax.psum(large_sums[2].astype(jnp.bfloat16), ("ctx", "dp")).astype(jnp.float32),
        lax.psum(large_sums[3].astype(jnp.bfloat16), ("ctx", "dp")).astype(jnp.float32),
        lax.psum(large_sums[4].astype(jnp.bfloat16), ("ctx", "dp")).astype(jnp.float32),
        lax.psum(large_sums[5].astype(jnp.bfloat16), ("ctx", "dp")).astype(jnp.float32),
        lax.psum(large_sums[6].astype(jnp.bfloat16), ("ctx", "dp")).astype(jnp.float32),
        lax.psum(large_sums[7].astype(jnp.bfloat16), ("ctx", "dp")).astype(jnp.float32),
    )
    small_sums = lax.psum(
        (conv_grad, score_grad, attn_gain_grad, bias_grad, ff_gain_grad), ("ctx", "dp", "ws")
    )
    return (
        output[None],
        byte_grad[None],
        large_sums[0],
        small_sums[0],
        small_sums[1],
        small_sums[2],
        large_sums[1],
        large_sums[2],
        large_sums[3],
        large_sums[4],
        small_sums[3],
        small_sums[4],
        large_sums[5],
        large_sums[6],
        large_sums[7],
    )


def solution(mesh):
    in_specs = (
        P(("dp", "ws"), "ctx"),
        P(("dp", "ws"), "ctx"),
        P(None, "ws"),
        P(),
        P(),
        P(),
        P("ws", None),
        P("ws", None),
        P("ws", None),
        P("ws", None),
        P(),
        P(),
        P("ws", None),
        P("ws", None),
        P("ws", None),
        P(("dp", "ws"), "ctx", None),
    )
    out_specs = (
        P(("dp", "ws"), "ctx", None),
        P(("dp", "ws"), "ctx", None),
        P(None, "ws"),
        P(),
        P(),
        P(),
        P("ws", None),
        P("ws", None),
        P("ws", None),
        P("ws", None),
        P(),
        P(),
        P("ws", None),
        P("ws", None),
        P("ws", None),
    )
    return jax.shard_map(
        per_device, mesh=mesh, in_specs=in_specs, out_specs=out_specs, check_vma=False
    )
```

profile of v0, /device:TPU:0, one launch (start us, length us, event | category | flops | bytes accessed | tf_op | source)
XLA Modules:
  0.0 2698.8 jit_solution(17159054184191954711)
XLA Ops:
  152.6 516.4 %while.44 = (s32[]{:T(128)}, bf16[12,504,64]{1,2,0:T(8,128)(2,1)S(1)}, f32[12,504]{1,0:T(8,128)S(1)}, s32[12]{0:T(128)S(1)}, bf16[504,768]{1,0:T(8,128)(2,1)}, /...) while((s32[]{:T(128)}, ...), condition=%wide.region_9.0_spmd.clone, body=%wide.region_6.10_spmd.clone.sunk | while | flops 276622912 | bytes 19570960 | solution.py:181
  717.7 849.8 %while.45 = (s32[]{:T(128)}, bf16[12,504,64]{1,2,0:T(8,128)(2,1)}, f32[12,32]{1,0:T(8,128)}, f32[12,504]{1,0:T(8,128)S(1)}, s32[12]{0:T(128)S(1)}, /*index=5*/bf...) while((s32[]{:T(128)}, bf16[12,504,64]{1,2,0:T(8,128)(2,1)}, ...), condition=%wide.region_15.17_spmd.clone, body=%wide.region_12.16_spmd.clone.sunk | while | flops 375602976 | bytes 66809256 | solution.py:250
  729.7 32.2 %multiply_reduce_fusion.18 = (f32[504]{0:T(512)S(1)}, f32[504,1512]{1,0:T(8,128)S(1)}) fusion(f32[504,1512]{1,0:T(8,128)S(1)} %fusion.295, f32[504]{0:T(512)S(1)} %bitcast.683, f32[]{:T(128)} %bitcast.544, f32[]{:T(128)} %bitcast.545, f32[]{:T(128)} %bitcast.546, f32[]{:T(128)} %bitcast.547, f32[]{:T(128)} %bitcast.548, f32[]{:T(128)} %bitcast.549, ...), kind=kOutput, calls=%fused_computation.57.clone.1 | convolution fusion | flops 176794624 | bytes 6649544 | tf_op jit(solution)/shard_map/while/body/eval_jaxpr/dot_general | solution.py:33
  800.5 32.2 %multiply_reduce_fusion.18 = (f32[504]{0:T(512)S(1)}, f32[504,1512]{1,0:T(8,128)S(1)}) fusion(f32[504,1512]{1,0:T(8,128)S(1)} %fusion.295, f32[504]{0:T(512)S(1)} %bitcast.683, f32[]{:T(128)} %bitcast.544, f32[]{:T(128)} %bitcast.545, f32[]{:T(128)} %bitcast.546, f32[]{:T(128)} %bitcast.547, f32[]{:T(128)} %bitcast.548, f32[]{:T(128)} %bitcast.549, ...), kind=kOutput, calls=%fused_computation.57.clone.1 | convolution fusion | flops 176794624 | bytes 6649544 | tf_op jit(solution)/shard_map/while/body/eval_jaxpr/dot_general | solution.py:33
  1366.7 32.2 %multiply_reduce_fusion.18 = (f32[504]{0:T(512)S(1)}, f32[504,1512]{1,0:T(8,128)S(1)}) fusion(f32[504,1512]{1,0:T(8,128)S(1)} %fusion.295, f32[504]{0:T(512)S(1)} %bitcast.683, f32[]{:T(128)} %bitcast.544, f32[]{:T(128)} %bitcast.545, f32[]{:T(128)} %bitcast.546, f32[]{:T(128)} %bitcast.547, f32[]{:T(128)} %bitcast.548, f32[]{:T(128)} %bitcast.549, ...), kind=kOutput, calls=%fused_computation.57.clone.1 | convolution fusion | flops 176794624 | bytes 6649544 | tf_op jit(solution)/shard_map/while/body/eval_jaxpr/dot_general | solution.py:33
  1508.2 32.2 %multiply_reduce_fusion.18 = (f32[504]{0:T(512)S(1)}, f32[504,1512]{1,0:T(8,128)S(1)}) fusion(f32[504,1512]{1,0:T(8,128)S(1)} %fusion.295, f32[504]{0:T(512)S(1)} %bitcast.683, f32[]{:T(128)} %bitcast.544, f32[]{:T(128)} %bitcast.545, f32[]{:T(128)} %bitcast.546, f32[]{:T(128)} %bitcast.547, f32[]{:T(128)} %bitcast.548, f32[]{:T(128)} %bitcast.549, ...), kind=kOutput, calls=%fused_computation.57.clone.1 | convolution fusion | flops 176794624 | bytes 6649544 | tf_op jit(solution)/shard_map/while/body/eval_jaxpr/dot_general | solution.py:33
  1581.9 577.3 %while.46 = (s32[]{:T(128)}, bf16[12,504,64]{1,2,0:T(8,128)(2,1)}, bf16[12,504,64]{1,2,0:T(8,128)(2,1)}, bf16[2,1512,768]{2,1,0:T(8,128)(2,1)}, s32[12]{0:T(128)...) while((s32[]{:T(128)}, bf16[12,504,64]{1,2,0:T(8,128)(2,1)}, ...), condition=%wide.region_17.19_spmd.clone.clone, body=%wide.region_16.18_spmd.clone.clone.sunk | while | flops 473993856 | bytes 20568888 | solution.py:270
  1592.1 32.9 %fusion.311 = f32[1512,504]{1,0:T(8,128)S(1)} fusion(s32[504]{0:T(512)S(1)} %get-tuple-element.1267, f32[]{:T(128)} %bitcast.611, f32[]{:T(128)} %bitcast.612, f32[]{:T(128)} %bitcast.613, f32[]{:T(128)} %bitcast.614, f32[]{:T(128)} %bitcast.615, f32[]{:T(128)} %bitcast.616, f32[]{:T(128)} %bitcast.617, f32[]{:T(128)} %bitcast.618, f32[]{:T(128)} %bitcast.619, ...), kind=kOutput, calls=%fused_computation.89.clone.1 | convolution fusion | flops 178319232 | bytes 3597320 | tf_op jit(solution)/shard_map/while/body/eval_jaxpr/dot_general | solution.py:33
  1640.2 32.9 %fusion.311 = f32[1512,504]{1,0:T(8,128)S(1)} fusion(s32[504]{0:T(512)S(1)} %get-tuple-element.1267, f32[]{:T(128)} %bitcast.611, f32[]{:T(128)} %bitcast.612, f32[]{:T(128)} %bitcast.613, f32[]{:T(128)} %bitcast.614, f32[]{:T(128)} %bitcast.615, f32[]{:T(128)} %bitcast.616, f32[]{:T(128)} %bitcast.617, f32[]{:T(128)} %bitcast.618, f32[]{:T(128)} %bitcast.619, ...), kind=kOutput, calls=%fused_computation.89.clone.1 | convolution fusion | flops 178319232 | bytes 3597320 | tf_op jit(solution)/shard_map/while/body/eval_jaxpr/dot_general | solution.py:33
  1688.3 32.9 %fusion.311 = f32[1512,504]{1,0:T(8,128)S(1)} fusion(s32[504]{0:T(512)S(1)} %get-tuple-element.1267, f32[]{:T(128)} %bitcast.611, f32[]{:T(128)} %bitcast.612, f32[]{:T(128)} %bitcast.613, f32[]{:T(128)} %bitcast.614, f32[]{:T(128)} %bitcast.615, f32[]{:T(128)} %bitcast.616, f32[]{:T(128)} %bitcast.617, f32[]{:T(128)} %bitcast.618, f32[]{:T(128)} %bitcast.619, ...), kind=kOutput, calls=%fused_computation.89.clone.1 | convolution fusion | flops 178319232 | bytes 3597320 | tf_op jit(solution)/shard_map/while/body/eval_jaxpr/dot_general | solution.py:33
  1736.4 32.9 %fusion.311 = f32[1512,504]{1,0:T(8,128)S(1)} fusion(s32[504]{0:T(512)S(1)} %get-tuple-element.1267, f32[]{:T(128)} %bitcast.611, f32[]{:T(128)} %bitcast.612, f32[]{:T(128)} %bitcast.613, f32[]{:T(128)} %bitcast.614, f32[]{:T(128)} %bitcast.615, f32[]{:T(128)} %bitcast.616, f32[]{:T(128)} %bitcast.617, f32[]{:T(128)} %bitcast.618, f32[]{:T(128)} %bitcast.619, ...), kind=kOutput, calls=%fused_computation.89.clone.1 | convolution fusion | flops 178319232 | bytes 3597320 | tf_op jit(solution)/shard_map/while/body/eval_jaxpr/dot_general | solution.py:33
  1784.5 32.9 %fusion.311 = f32[1512,504]{1,0:T(8,128)S(1)} fusion(s32[504]{0:T(512)S(1)} %get-tuple-element.1267, f32[]{:T(128)} %bitcast.611, f32[]{:T(128)} %bitcast.612, f32[]{:T(128)} %bitcast.613, f32[]{:T(128)} %bitcast.614, f32[]{:T(128)} %bitcast.615, f32[]{:T(128)} %bitcast.616, f32[]{:T(128)} %bitcast.617, f32[]{:T(128)} %bitcast.618, f32[]{:T(128)} %bitcast.619, ...), kind=kOutput, calls=%fused_computation.89.clone.1 | convolution fusion | flops 178319232 | bytes 3597320 | tf_op jit(solution)/shard_map/while/body/eval_jaxpr/dot_general | solution.py:33
  1832.6 32.9 %fusion.311 = f32[1512,504]{1,0:T(8,128)S(1)} fusion(s32[504]{0:T(512)S(1)} %get-tuple-element.1267, f32[]{:T(128)} %bitcast.611, f32[]{:T(128)} %bitcast.612, f32[]{:T(128)} %bitcast.613, f32[]{:T(128)} %bitcast.614, f32[]{:T(128)} %bitcast.615, f32[]{:T(128)} %bitcast.616, f32[]{:T(128)} %bitcast.617, f32[]{:T(128)} %bitcast.618, f32[]{:T(128)} %bitcast.619, ...), kind=kOutput, calls=%fused_computation.89.clone.1 | convolution fusion | flops 178319232 | bytes 3597320 | tf_op jit(solution)/shard_map/while/body/eval_jaxpr/dot_general | solution.py:33
  1880.7 32.9 %fusion.311 = f32[1512,504]{1,0:T(8,128)S(1)} fusion(s32[504]{0:T(512)S(1)} %get-tuple-element.1267, f32[]{:T(128)} %bitcast.611, f32[]{:T(128)} %bitcast.612, f32[]{:T(128)} %bitcast.613, f32[]{:T(128)} %bitcast.614, f32[]{:T(128)} %bitcast.615, f32[]{:T(128)} %bitcast.616, f32[]{:T(128)} %bitcast.617, f32[]{:T(128)} %bitcast.618, f32[]{:T(128)} %bitcast.619, ...), kind=kOutput, calls=%fused_computation.89.clone.1 | convolution fusion | flops 178319232 | bytes 3597320 | tf_op jit(solution)/shard_map/while/body/eval_jaxpr/dot_general | solution.py:33
  1928.8 32.9 %fusion.311 = f32[1512,504]{1,0:T(8,128)S(1)} fusion(s32[504]{0:T(512)S(1)} %get-tuple-element.1267, f32[]{:T(128)} %bitcast.611, f32[]{:T(128)} %bitcast.612, f32[]{:T(128)} %bitcast.613, f32[]{:T(128)} %bitcast.614, f32[]{:T(128)} %bitcast.615, f32[]{:T(128)} %bitcast.616, f32[]{:T(128)} %bitcast.617, f32[]{:T(128)} %bitcast.618, f32[]{:T(128)} %bitcast.619, ...), kind=kOutput, calls=%fused_computation.89.clone.1 | convolution fusion | flops 178319232 | bytes 3597320 | tf_op jit(solution)/shard_map/while/body/eval_jaxpr/dot_general | solution.py:33
  1976.9 32.9 %fusion.311 = f32[1512,504]{1,0:T(8,128)S(1)} fusion(s32[504]{0:T(512)S(1)} %get-tuple-element.1267, f32[]{:T(128)} %bitcast.611, f32[]{:T(128)} %bitcast.612, f32[]{:T(128)} %bitcast.613, f32[]{:T(128)} %bitcast.614, f32[]{:T(128)} %bitcast.615, f32[]{:T(128)} %bitcast.616, f32[]{:T(128)} %bitcast.617, f32[]{:T(128)} %bitcast.618, f32[]{:T(128)} %bitcast.619, ...), kind=kOutput, calls=%fused_computation.89.clone.1 | convolution fusion | flops 178319232 | bytes 3597320 | tf_op jit(solution)/shard_map/while/body/eval_jaxpr/dot_general | solution.py:33
  2025.0 32.9 %fusion.311 = f32[1512,504]{1,0:T(8,128)S(1)} fusion(s32[504]{0:T(512)S(1)} %get-tuple-element.1267, f32[]{:T(128)} %bitcast.611, f32[]{:T(128)} %bitcast.612, f32[]{:T(128)} %bitcast.613, f32[]{:T(128)} %bitcast.614, f32[]{:T(128)} %bitcast.615, f32[]{:T(128)} %bitcast.616, f32[]{:T(128)} %bitcast.617, f32[]{:T(128)} %bitcast.618, f32[]{:T(128)} %bitcast.619, ...), kind=kOutput, calls=%fused_computation.89.clone.1 | convolution fusion | flops 178319232 | bytes 3597320 | tf_op jit(solution)/shard_map/while/body/eval_jaxpr/dot_general | solution.py:33
  2073.1 32.9 %fusion.311 = f32[1512,504]{1,0:T(8,128)S(1)} fusion(s32[504]{0:T(512)S(1)} %get-tuple-element.1267, f32[]{:T(128)} %bitcast.611, f32[]{:T(128)} %bitcast.612, f32[]{:T(128)} %bitcast.613, f32[]{:T(128)} %bitcast.614, f32[]{:T(128)} %bitcast.615, f32[]{:T(128)} %bitcast.616, f32[]{:T(128)} %bitcast.617, f32[]{:T(128)} %bitcast.618, f32[]{:T(128)} %bitcast.619, ...), kind=kOutput, calls=%fused_computation.89.clone.1 | convolution fusion | flops 178319232 | bytes 3597320 | tf_op jit(solution)/shard_map/while/body/eval_jaxpr/dot_general | solution.py:33
  2121.2 32.9 %fusion.311 = f32[1512,504]{1,0:T(8,128)S(1)} fusion(s32[504]{0:T(512)S(1)} %get-tuple-element.1267, f32[]{:T(128)} %bitcast.611, f32[]{:T(128)} %bitcast.612, f32[]{:T(128)} %bitcast.613, f32[]{:T(128)} %bitcast.614, f32[]{:T(128)} %bitcast.615, f32[]{:T(128)} %bitcast.616, f32[]{:T(128)} %bitcast.617, f32[]{:T(128)} %bitcast.618, f32[]{:T(128)} %bitcast.619, ...), kind=kOutput, calls=%fused_computation.89.clone.1 | convolution fusion | flops 178319232 | bytes 3597320 | tf_op jit(solution)/shard_map/while/body/eval_jaxpr/dot_general | solution.py:33
  2375.8 46.3 %reduce-scatter.19.cloned.1.call-done = bf16[384,2048]{1,0:T(8,128)(2,1)} async-done(((bf16[768,2048]{1,0:T(8,128)(2,1)}), bf16[384,2048]{1,0:T(8,128)(2,1)}) %reduce-scatter.19.cloned.1.call-update) | async-done | bytes 1572880 | tf_op jit(solution)/shard_map/reduce_scatter | solution.py:343
  2422.0 46.1 %reduce-scatter.21.cloned.1.call-done = bf16[384,2048]{1,0:T(8,128)(2,1)} async-done(((bf16[768,2048]{1,0:T(8,128)(2,1)}), bf16[384,2048]{1,0:T(8,128)(2,1)}) %reduce-scatter.21.cloned.1.call-update) | async-done | bytes 1572880 | tf_op jit(solution)/shard_map/reduce_scatter | solution.py:346
  2468.1 46.1 %reduce-scatter.23.cloned.1.call-done = bf16[1024,768]{1,0:T(8,128)(2,1)} async-done(((bf16[2048,768]{1,0:T(8,128)(2,1)}), bf16[1024,768]{1,0:T(8,128)(2,1)}) %reduce-scatter.23.cloned.1.call-update) | async-done | bytes 1572880 | tf_op jit(solution)/shard_map/reduce_scatter | solution.py:349
  2530.9 41.9 %all-reduce.2 = (f32[5,768]{1,0:T(8,128)}, f32[768]{0:T(1024)}, f32[768]{0:T(1024)}, f32[32,12]{0,1:T(8,128)}, f32[768]{0:T(1024)}) all-reduce(f32[5,768]{1,0:T(8,128)S(1)} %stack.103, f32[768]{0:T(1024)S(1)} %add_add_fusion.2, f32[768]{0:T(1024)S(1)} %get-tuple-element.428, ...), channel_id=1, replica_groups=mesh['ctx'=8,'dp'=2,'ws'=2] {'ctx','dp','ws'}, use_global_device_ids=true, to_apply=%region_35.37 | all-reduce | flops 6528 | bytes 52224 | tf_op jit(solution)/shard_map/psum | solution.py:363
  2575.7 102.0 %all-reduce.6.cloned.1.call-done = (bf16[259,384]{1,0:T(8,128)(2,1)}, bf16[384,768]{1,0:T(8,128)(2,1)}, bf16[384,768]{1,0:T(8,128)(2,1)}, bf16[384,768]{1,0:T(8,...) async-done(((bf16[259,384]{1,0:T(8,128)(2,1)}, bf16[384,768]{1,0:T(8,128)(2,1)}, ...) | async-done | bytes 7276816 | tf_op jit(solution)/shard_map/psum | solution.py:354
  (826 shorter events, 1781.1 us)
Async XLA Ops:
  7.2 112.4 %all-gather.12.cloned.1.call-start = ((), (), s32[]{:S(2)}) async-start(), calls=%async_computation.10 | async-start | bytes 1769472 | tf_op jit(solution)/shard_map/all_gather | solution.py:123
  8.0 114.3 %all-gather.10.cloned.1.call-start = ((), (), s32[]{:S(2)}) async-start(), calls=%async_computation.9 | async-start | bytes 1769472 | tf_op jit(solution)/shard_map/all_gather | solution.py:122
  8.7 136.8 %all-gather.8.cloned.1.call-start = ((), (), s32[]{:S(2)}) async-start(), calls=%async_computation.8 | async-start | bytes 1769472 | tf_op jit(solution)/shard_map/all_gather | solution.py:121
  9.5 659.6 %all-gather.14.cloned.1.call-start = ((), (), s32[]{:S(2)}) async-start(), calls=%async_computation.11 | async-start | bytes 1769472 | tf_op jit(solution)/shard_map/all_gather | solution.py:124
  10.0 662.2 %all-gather.16.cloned.1.call-start = ((), (), s32[]{:S(2)}) async-start(), calls=%async_computation.12 | async-start | bytes 4718592 | tf_op jit(solution)/shard_map/all_gather | solution.py:125
  10.6 668.5 %all-gather.18.cloned.1.call-start = ((), (), s32[]{:S(2)}) async-start(), calls=%async_computation.13 | async-start | bytes 4718592 | tf_op jit(solution)/shard_map/all_gather | solution.py:126
  10.7 13.1 collective-permute-start
  13.1 10.7 collective-permute-start.1
  14.4 670.6 %all-gather.20.cloned.1.call-start = ((), (), s32[]{:S(2)}) async-start(), calls=%async_computation.14 | async-start | bytes 4718592 | tf_op jit(solution)/shard_map/all_gather | solution.py:127
  126.3 22.4 collective-permute-start.3
  127.6 21.1 collective-permute-start.2
  135.2 2152.6 %reduce-scatter.25.cloned.1.call-start = ((), (), s32[]{:S(2)}) async-start(), calls=%async_computation.22 | async-start | bytes 884736
  704.2 871.9 %collective-permute-start.5 = (bf16[2,504,768]{2,1,0:T(8,128)(2,1)}, bf16[2,504,768]{2,1,0:T(8,128)(2,1)}, u32[]{:S(2)}, u32[]{:S(2)}) collective-permute-start(bf16[2,504,768]{2,1,0:T(8,128)(2,1)} %pad_maximum_fusion.3), channel_id=1, source_target_pairs={{4,0},{8,4},{12,8},{16,12},{20,16},{24,20},{28,24},{5,1},{9,5},{13... | collective-permute-start | bytes 4644872 | tf_op jit(solution)/shard_map/ppermute | solution.py:20
  705.4 870.6 %collective-permute-start.4 = (bf16[2,504,768]{2,1,0:T(8,128)(2,1)}, bf16[2,504,768]{2,1,0:T(8,128)(2,1)}, u32[]{:S(2)}, u32[]{:S(2)}) collective-permute-start(bf16[2,504,768]{2,1,0:T(8,128)(2,1)} %pad_maximum_fusion.3), channel_id=1, source_target_pairs={{0,4},{4,8},{8,12},{12,16},{16,20},{20,24},{24,28},{1,5},{5,9},{9,... | collective-permute-start | bytes 4644872 | tf_op jit(solution)/shard_map/ppermute | solution.py:17
  1567.6 8.3 collective-permute-start.6
  2243.5 5.5 collective-permute-start.9
  2257.6 44.6 %reduce-scatter.11.cloned.1.call-start = ((), (), s32[]{:S(2)}) async-start(), calls=%async_computation.15 | async-start | bytes 1769472 | tf_op jit(solution)/shard_map/reduce_scatter | solution.py:331
  2260.9 65.7 %reduce-scatter.17.cloned.1.call-start = ((), (), s32[]{:S(2)}) async-start(), calls=%async_computation.18 | async-start | bytes 1769472 | tf_op jit(solution)/shard_map/reduce_scatter | solution.py:340
  2264.8 86.5 %reduce-scatter.13.cloned.1.call-start = ((), (), s32[]{:S(2)}) async-start(), calls=%async_computation.16 | async-start | bytes 1769472 | tf_op jit(solution)/shard_map/reduce_scatter | solution.py:334
  2268.1 107.7 %reduce-scatter.15.cloned.1.call-start = ((), (), s32[]{:S(2)}) async-start(), calls=%async_computation.17 | async-start | bytes 1769472 | tf_op jit(solution)/shard_map/reduce_scatter | solution.py:337
  2271.4 150.7 %reduce-scatter.19.cloned.1.call-start = ((), (), s32[]{:S(2)}) async-start(), calls=%async_computation.19 | async-start | bytes 4718592 | tf_op jit(solution)/shard_map/reduce_scatter | solution.py:343
  2276.8 191.3 %reduce-scatter.21.cloned.1.call-start = ((), (), s32[]{:S(2)}) async-start(), calls=%async_computation.20 | async-start | bytes 4718592 | tf_op jit(solution)/shard_map/reduce_scatter | solution.py:346
  2282.2 232.0 %reduce-scatter.23.cloned.1.call-start = ((), (), s32[]{:S(2)}) async-start(), calls=%async_computation.21 | async-start | bytes 4718592 | tf_op jit(solution)/shard_map/reduce_scatter | solution.py:349
  2287.5 390.1 %all-reduce.6.cloned.1.call-start = ((), (), s32[]{:S(2)}) async-start(), calls=%async_computation.23 | async-start | bytes 14561280 | tf_op jit(solution)/shard_map/psum | solution.py:354
  (88 other events, 969.7 us)
Sparse Core Ops, SparseCore 0:
  9.6 26.7 all-gather.11
  37.9 24.9 all-gather.9
  64.4 22.7 all-gather.7
  88.7 22.7 all-gather.13
  112.9 44.9 all-gather.15
  159.2 44.9 all-gather.17
  205.7 44.9 all-gather.19
  2257.7 19.7 reduce-scatter.24
  2280.4 21.7 reduce-scatter.10
  2304.8 21.7 reduce-scatter.16
  2329.5 21.7 reduce-scatter.12
  2354.0 21.7 reduce-scatter.14
  2378.7 43.3 reduce-scatter.18
  2424.7 43.3 reduce-scatter.20
  2470.8 43.3 reduce-scatter.22
  2519.3 158.3 all-reduce.5
where the time goes:
time: 2730 us; the launch traced here: 2700 us
  matrix products  1400 us (51%)
  local copies, waits for them, and re-layouts  626 us (23%)
  waiting for transfers between devices  330 us (12%)
  other arithmetic  140 us (5%)
  loops' own time  96.1 us (4%)
  blocking collectives  50.5 us (2%)
  starting transfers between devices  36.3 us (1%)
    dot_general x86, matrix products, contract(): lax.dot_general(left_side, right_side, (((left_axis,), (right_axis,)), ((...  1300 us
    psum x1, waiting for transfers between devices, per_device(): lax.psum(large_sums[0].astype(jnp.bfloat16), ('ctx', 'dp'))  102 us
    reshape x12, local copies, waits for them, and re-layouts, diagonal_sums(): skewed = flat_grid.reshape(row_total, col_total + row_total + 1)  82.8 us
    reshape x12, local copies, waits for them, and re-layouts, diagonal_sums(): flat_grid = jnp.pad(wider_grid.reshape(-1), (0, row_total))  73.2 us
    slice x12, local copies, waits for them, and re-layouts, key_head(): grad_part = head_slice(query_rim[1], head_number, head_dim)  57.7 us
    slice x12, local copies, waits for them, and re-layouts, score_grads(): value_part = head_slice(key_value[1], head_number, head_dim)  57.7 us
  transfers between devices with their start and end apart: 26, of which 9 were waited for; matrix products, arithmetic and copies ran while one was open for 55% of the time, Pallas kernels for 0%

commit v1 on v0

--- a/solution.py
+++ b/solution.py
@@ -1,12 +1,414 @@
+import functools
+
 import jax
 import jax.numpy as jnp
 from jax import lax
+from jax.experimental import pallas as pl
+from jax.experimental.pallas import tpu as pltpu
 from jax.sharding import PartitionSpec as P
 
 thresholds = (12, 16, 23, 32, 46, 64, 91)
 negative = -1e30
 epsilon = 1e-06
 highest = lax.Precision.HIGHEST
+tile = 128
+near_bases = (-128, -120, 0, 120, 128)
+class_count = len(near_bases) + 2
+
+
+def bucket_of(relative):
+    distance = jnp.abs(relative)
+    far_bucket = 8 + sum(((distance >= threshold).astype(jnp.int32) for threshold in thresholds))
+    near_bucket = jnp.where(distance < 8, distance, far_bucket)
+    return near_bucket + 16 * (relative > 0).astype(jnp.int32)
+
+
+def matmul(left, right, left_dim, right_dim):
+    return lax.dot_general(
+        left, right, (((left_dim,), (right_dim,)), ((), ())), preferred_element_type=jnp.float32
+    )
+
+
+def split_pair(values):
+    high = values.astype(jnp.bfloat16)
+    return high, (values - high.astype(jnp.float32)).astype(jnp.bfloat16)
+
+
+def tile_class(query_tile, key_tile):
+    step = key_tile - query_tile - 4
+    own = jnp.where(
+        step <= -2, 0, jnp.where(step == -1, 1, jnp.where(step == 0, 3, jnp.where(step == 1, 5, 6)))
+    )
+    before = jnp.where(step == -1, 2, 0)
+    after = jnp.where(step == 1, 4, 6)
+    return jnp.where(key_tile < 4, before, jnp.where(key_tile < 8, own, after))
+
+
+def key_range(seg_ref, query_tile, row_count, tiles_per_block):
+    first_seg = seg_ref[1, query_tile * tile]
+    last_seg = seg_ref[1, jnp.minimum(query_tile * tile + tile, row_count) - 1]
+    low = jnp.int32(0)
+    high = jnp.int32(0)
+    for block in range(3):
+        for part in range(tiles_per_block):
+            key_first = seg_ref[block, part * tile]
+            key_last = seg_ref[block, min(part * tile + tile, row_count) - 1]
+            low = low + (key_last < first_seg).astype(jnp.int32)
+            high = high + (key_first <= last_seg).astype(jnp.int32)
+    return low, high
+
+
+def make_bias(line_ref, bias_ref, pair_count):
+    for kind in range(class_count):
+        for pair in range(pair_count):
+            for half in range(2):
+                head = 2 * pair + half
+                line = line_ref[kind, head : head + 1, :]
+                grid = jnp.broadcast_to(line, (tile, 2 * tile))
+                if 0 < kind < class_count - 1:
+                    grid = pltpu.roll(grid, 0, 1, stride=1, stride_axis=0)
+                bias_ref[kind, pair, :, half * tile : (half + 1) * tile] = grid[:, :tile]
+
+
+def stack_heads(block):
+    lane = lax.broadcasted_iota(jnp.int32, block.shape, 1)
+    zero = jnp.zeros_like(block)
+    return jnp.concatenate(
+        [jnp.where(lane < tile // 2, block, zero), jnp.where(lane < tile // 2, zero, block)], axis=0
+    )
+
+
+def fold_rows(values, combine):
+    pieces = [values[8 * i : 8 * i + 8] for i in range(values.shape[0] // 8)]
+    while len(pieces) > 1:
+        joined = [combine(pieces[i], pieces[i + 1]) for i in range(0, len(pieces) - 1, 2)]
+        if len(pieces) % 2:
+            joined.append(pieces[-1])
+        pieces = joined
+    return pieces[0]
+
+
+def key_columns(segs_ref, column_ref, key_tile):
+    row = segs_ref[key_tile, 0:1, :]
+    column_ref[key_tile] = jnp.transpose(jnp.broadcast_to(row, (tile, tile)))
+
+
+def start_copies(sources, window_ref, sems):
+    rows = sources[0].shape[0]
+    copies = [
+        pltpu.make_async_copy(source, window_ref.at[pl.ds(rows * i, rows)], sems.at[i])
+        for i, source in enumerate(sources)
+    ]
+    for copy in copies:
+        copy.start()
+    return copies
+
+
+def forward_kernel(
+    seg_ref, q_ref, before_ref, own_ref, after_ref, segs_ref, qsegs_ref, line_ref,
+    out_ref, lse_ref,
+    window_ref, bias_ref, column_ref, mask_ref, flipped_ref, score_ref, mixed_ref, sems, *, row_count
+):
+    width = q_ref.shape[1]
+    pair_count = width // tile
+    query_tiles = q_ref.shape[0] // tile
+    copies = start_copies((before_ref, own_ref, after_ref), window_ref, sems)
+    make_bias(line_ref, bias_ref, pair_count)
+    first = key_range(seg_ref, 0, row_count, query_tiles)[0]
+    last = key_range(seg_ref, query_tiles - 1, row_count, query_tiles)[1]
+    for copy in copies:
+        copy.wait()
+
+    def prepare(key_tile, carry):
+        key_columns(segs_ref, column_ref, key_tile)
+        at = pl.multiple_of(key_tile * tile, tile)
+        flipped_ref[key_tile] = jnp.transpose(window_ref[pl.ds(at, tile), width:])
+        return carry
+
+    lax.fori_loop(first, last, prepare, 0)
+
+    def query_step(query_tile, carry):
+        low, high = key_range(seg_ref, query_tile, row_count, query_tiles)
+        rows = pl.ds(pl.multiple_of(query_tile * tile, tile), tile)
+        stacked = [
+            stack_heads(q_ref[rows, pair * tile : (pair + 1) * tile]) for pair in range(pair_count)
+        ]
+        query_seg = qsegs_ref[query_tile, 0:1, :]
+
+        def score_step(key_tile, tops):
+            keys = pl.ds(pl.multiple_of(key_tile * tile, tile), tile)
+            hide = jnp.where(column_ref[key_tile] == query_seg, 0.0, negative)
+            hide = jnp.concatenate([hide, hide], axis=1)
+            kind = tile_class(query_tile, key_tile)
+            fresh = []
+            for pair in range(pair_count):
+                scores = matmul(
+                    window_ref[keys, pair * tile : (pair + 1) * tile], stacked[pair], 1, 1
+                )
+                scores = scores + bias_ref[kind, pair] + hide
+                score_ref[key_tile, pair] = scores
+                fresh.append(jnp.maximum(tops[pair], fold_rows(scores, jnp.maximum)))
+            return tuple(fresh)
+
+        tops = lax.fori_loop(
+            low, high, score_step,
+            tuple(jnp.full((8, 2 * tile), negative, jnp.float32) for _ in range(pair_count)),
+        )
+        tops = [jnp.max(top, axis=0, keepdims=True) for top in tops]
+        for pair in range(pair_count):
+            mixed_ref[pair] = jnp.zeros((tile, tile), jnp.float32)
+
+        def mix_step(key_tile, totals):
+            fresh = []
+            for pair in range(pair_count):
+                exponent = jnp.exp(score_ref[key_tile, pair] - tops[pair])
+                fresh.append(totals[pair] + fold_rows(exponent, jnp.add))
+                mixed = matmul(
+                    flipped_ref[key_tile, pair * tile : (pair + 1) * tile, :],
+                    exponent.astype(jnp.bfloat16), 1, 0,
+                )
+                half = tile // 2
+                mixed_ref[pair, :half] += mixed[:half, :tile]
+                mixed_ref[pair, half:] += mixed[half:, tile:]
+            return tuple(fresh)
+
+        totals = lax.fori_loop(
+            low, high, mix_step,
+            tuple(jnp.zeros((8, 2 * tile), jnp.float32) for _ in range(pair_count)),
+        )
+        for pair in range(pair_count):
+            total = jnp.sum(totals[pair], axis=0, keepdims=True)
+            lse_ref[query_tile, pair : pair + 1, :] = tops[pair] + jnp.log(total)
+            inverse = 1.0 / total
+            half = tile // 2
+            scaled = jnp.concatenate(
+                [
+                    mixed_ref[pair, :half] * inverse[:, :tile],
+                    mixed_ref[pair, half:] * inverse[:, tile:],
+                ],
+                axis=0,
+            )
+            out_ref[rows, pair * tile : (pair + 1) * tile] = jnp.transpose(scaled).astype(
+                jnp.bfloat16
+            )
+        return carry
+
+    lax.fori_loop(0, query_tiles, query_step, 0)
+
+
+def backward_kernel(
+    seg_ref, q_ref, do_ref, o_ref, before_ref, own_ref, after_ref, segs_ref, qsegs_ref, line_ref, lse_ref,
+    dq_ref, dbefore_ref, down_ref, dafter_ref, bias_out_ref,
+    window_ref, bias_ref, column_ref, flipped_ref, dbias_ref, dwindow_ref, dq_acc_ref, delta_ref, sems,
+    *, row_count
+):
+    width = q_ref.shape[1]
+    pair_count = width // tile
+    query_tiles = q_ref.shape[0] // tile
+    block_rows = q_ref.shape[0]
+    half = tile // 2
+    copies = start_copies((before_ref, own_ref, after_ref), window_ref, sems)
+    make_bias(line_ref, bias_ref, pair_count)
+    dwindow_ref[...] = jnp.zeros(dwindow_ref.shape, jnp.float32)
+    dbias_ref[...] = jnp.zeros(dbias_ref.shape, jnp.float32)
+    product = do_ref[...].astype(jnp.float32) * o_ref[...].astype(jnp.float32)
+    product_high, product_low = split_pair(product)
+    member = (
+        lax.broadcasted_iota(jnp.int32, (16, width), 1) // half
+        == lax.broadcasted_iota(jnp.int32, (16, width), 0)
+    ).astype(jnp.bfloat16)
+    delta_ref[...] = matmul(member, product_high, 1, 1) + matmul(member, product_low, 1, 1)
+    first = key_range(seg_ref, 0, row_count, query_tiles)[0]
+    last = key_range(seg_ref, query_tiles - 1, row_count, query_tiles)[1]
+    for copy in copies:
+        copy.wait()
+
+    def prepare(key_tile, carry):
+        key_columns(segs_ref, column_ref, key_tile)
+        at = pl.multiple_of(key_tile * tile, tile)
+        flipped_ref[key_tile] = jnp.transpose(window_ref[pl.ds(at, tile), :width])
+        return carry
+
+    lax.fori_loop(first, last, prepare, 0)
+
+    def query_step(query_tile, carry):
+        low, high = key_range(seg_ref, query_tile, row_count, query_tiles)
+        at = pl.multiple_of(query_tile * tile, tile)
+        rows = pl.ds(at, tile)
+        lanes = [slice(pair * tile, (pair + 1) * tile) for pair in range(pair_count)]
+        queries = [stack_heads(q_ref[rows, lane]) for lane in lanes]
+        grads = [stack_heads(do_ref[rows, lane]) for lane in lanes]
+        query_seg = qsegs_ref[query_tile, 0:1, :]
+        deltas = [
+            jnp.concatenate(
+                [delta_ref[2 * pair : 2 * pair + 1, rows], delta_ref[2 * pair + 1 : 2 * pair + 2, rows]],
+                axis=1,
+            )
+            for pair in range(pair_count)
+        ]
+        norms = [lse_ref[query_tile, pair : pair + 1, :] for pair in range(pair_count)]
+        for pair in range(pair_count):
+            dq_acc_ref[pair] = jnp.zeros((tile, tile), jnp.float32)
+
+        def key_step(key_tile, carry):
+            keys = pl.ds(pl.multiple_of(key_tile * tile, tile), tile)
+            hide = jnp.where(column_ref[key_tile] == query_seg, 0.0, negative)
+            hide = jnp.concatenate([hide, hide], axis=1)
+            kind = tile_class(query_tile, key_tile)
+            for pair in range(pair_count):
+                lane = lanes[pair]
+                value_lane = slice(width + pair * tile, width + (pair + 1) * tile)
+                scores = matmul(window_ref[keys, lane], queries[pair], 1, 1)
+                probs = jnp.exp(scores + bias_ref[kind, pair] + hide - norms[pair])
+                dprobs = matmul(window_ref[keys, value_lane], grads[pair], 1, 1)
+                dscores = probs * (dprobs - deltas[pair])
+                dbias_ref[kind, pair] += dscores
+                dscores_low = dscores.astype(jnp.bfloat16)
+                dwindow_ref[keys, lane] += matmul(dscores_low, queries[pair], 1, 0)
+                dwindow_ref[keys, value_lane] += matmul(
+                    probs.astype(jnp.bfloat16), grads[pair], 1, 0
+                )
+                dquery = matmul(flipped_ref[key_tile, lane, :], dscores_low, 1, 0)
+                dq_acc_ref[pair, :half] += dquery[:half, :tile]
+                dq_acc_ref[pair, half:] += dquery[half:, tile:]
+            return carry
+
+        lax.fori_loop(low, high, key_step, 0)
+        for pair in range(pair_count):
+            dq_ref[rows, lanes[pair]] = jnp.transpose(dq_acc_ref[pair]).astype(jnp.bfloat16)
+        return carry
+
+    lax.fori_loop(0, query_tiles, query_step, 0)
+    dbefore_ref[...] = dwindow_ref[:block_rows].astype(jnp.bfloat16)
+    down_ref[...] = dwindow_ref[block_rows : 2 * block_rows]
+    dafter_ref[...] = dwindow_ref[2 * block_rows :].astype(jnp.bfloat16)
+    turn = (
+        lax.broadcasted_iota(jnp.int32, (tile, tile), 0)
+        + lax.broadcasted_iota(jnp.int32, (tile, tile), 1)
+        == tile - 1
+    ).astype(jnp.bfloat16)
+    zero_half = jnp.zeros((tile, tile), jnp.float32)
+    bias_out_ref[...] = jnp.zeros(bias_out_ref.shape, jnp.float32)
+    for kind in range(class_count):
+        for pair in range(pair_count):
+            grid = dbias_ref[kind, pair]
+            near = 0 < kind < class_count - 1
+            if near:
+                grid_high, grid_low = split_pair(grid)
+                grid = matmul(turn, grid_high, 1, 0) + matmul(turn, grid_low, 1, 0)
+            for side in range(2):
+                part = jnp.concatenate([grid[:, side * tile : (side + 1) * tile], zero_half], axis=1)
+                if near:
+                    part = pltpu.roll(part, tile + 1, 1, stride=1, stride_axis=0)
+                head = 2 * pair + side
+                bias_out_ref[kind, head : head + 1, :] = jnp.sum(
+                    fold_rows(part, jnp.add), axis=0, keepdims=True
+                )
+
+
+def line_offsets():
+    place = jnp.arange(2 * tile, dtype=jnp.int32)
+    swing = jnp.where(place < tile, place, place - 2 * tile)
+    far = jnp.full((1, 2 * tile), 4 * tile, jnp.int32)
+    near = jnp.stack([base - swing for base in near_bases])
+    return jnp.concatenate([-far, near, far])
+
+
+def bias_lines(rel_bias):
+    bucket_count, head_count = rel_bias.shape
+    buckets = bucket_of(line_offsets())
+    lines = jnp.take(rel_bias, buckets.reshape(-1), axis=0).reshape(class_count, 2 * tile, head_count)
+    lines = jnp.transpose(lines, (0, 2, 1))
+    return jnp.pad(lines, ((0, 0), (0, 16 - head_count), (0, 0)))
+
+
+def bias_collect(sums, bucket_count, head_count):
+    onehot = (bucket_of(line_offsets())[:, :, None] == jnp.arange(bucket_count)).astype(jnp.float32)
+    return jnp.einsum(
+        "chx,cxb->bh", sums[:, :head_count], onehot, precision=lax.Precision.HIGHEST
+    )
+
+
+def specs(count, space=pltpu.VMEM):
+    return [pl.BlockSpec(memory_space=space) for _ in range(count)]
+
+
+def attention_forward(segs, q, before, own, after, lines, row_count):
+    rows, width = q.shape
+    tiles = rows // tile
+    pairs = width // tile
+    seg_rows = segs.reshape(3 * tiles, 1, tile)
+    query_segs = mark_queries(segs, row_count).reshape(tiles, 1, tile)
+    return pl.pallas_call(
+        functools.partial(forward_kernel, row_count=row_count),
+        out_shape=(
+            jax.ShapeDtypeStruct((rows, width), jnp.bfloat16),
+            jax.ShapeDtypeStruct((tiles, 8, 2 * tile), jnp.float32),
+        ),
+        in_specs=specs(1, pltpu.SMEM) + specs(1) + specs(3, pl.ANY) + specs(3),
+        out_specs=tuple(specs(2)),
+        scratch_shapes=[
+            pltpu.VMEM((3 * rows, 2 * width), jnp.bfloat16),
+            pltpu.VMEM((class_count, pairs, tile, 2 * tile), jnp.float32),
+            pltpu.VMEM((3 * tiles, tile, tile), jnp.int32),
+            pltpu.VMEM((8, 128), jnp.float32),
+            pltpu.VMEM((3 * tiles, width, tile), jnp.bfloat16),
+            pltpu.VMEM((3 * tiles, pairs, tile, 2 * tile), jnp.float32),
+            pltpu.VMEM((pairs, tile, tile), jnp.float32),
+            pltpu.SemaphoreType.DMA((3,)),
+        ],
+        compiler_params=pltpu.CompilerParams(vmem_limit_bytes=60 << 20),
+        name="attention_forward",
+    )(segs, q, before, own, after, seg_rows, query_segs, lines)
+
+
+def mark_queries(segs, row_count):
+    place = jnp.arange(segs.shape[1], dtype=jnp.int32)
+    return jnp.where(place < row_count, segs[1], -1)
+
+
+def attention_backward(segs, q, do, o, before, own, after, lines, lse, row_count):
+    rows, width = q.shape
+    tiles = rows // tile
+    pairs = width // tile
+    seg_rows = segs.reshape(3 * tiles, 1, tile)
+    query_segs = mark_queries(segs, row_count).reshape(tiles, 1, tile)
+    return pl.pallas_call(
+        functools.partial(backward_kernel, row_count=row_count),
+        out_shape=(
+            jax.ShapeDtypeStruct((rows, width), jnp.bfloat16),
+            jax.ShapeDtypeStruct((rows, 2 * width), jnp.bfloat16),
+            jax.ShapeDtypeStruct((rows, 2 * width), jnp.float32),
+            jax.ShapeDtypeStruct((rows, 2 * width), jnp.bfloat16),
+            jax.ShapeDtypeStruct((class_count, 16, 2 * tile), jnp.float32),
+        ),
+        in_specs=specs(1, pltpu.SMEM) + specs(3) + specs(3, pl.ANY) + specs(4),
+        out_specs=tuple(specs(5)),
+        scratch_shapes=[
+            pltpu.VMEM((3 * rows, 2 * width), jnp.bfloat16),
+            pltpu.VMEM((class_count, pairs, tile, 2 * tile), jnp.float32),
+            pltpu.VMEM((3 * tiles, tile, tile), jnp.int32),
+            pltpu.VMEM((3 * tiles, width, tile), jnp.bfloat16),
+            pltpu.VMEM((class_count, pairs, tile, 2 * tile), jnp.float32),
+            pltpu.VMEM((3 * rows, 2 * width), jnp.float32),
+            pltpu.VMEM((pairs, tile, tile), jnp.float32),
+            pltpu.VMEM((16, rows), jnp.float32),
+            pltpu.SemaphoreType.DMA((3,)),
+        ],
+        compiler_params=pltpu.CompilerParams(vmem_limit_bytes=60 << 20),
+        name="attention_backward",
+    )(segs, q, do, o, before, own, after, seg_rows, query_segs, lines, lse)
+
+
+def neighbours(block, axis):
+    count = lax.axis_size(axis)
+    forward = [(i, i + 1) for i in range(count - 1)]
+    backward = [(target, source) for source, target in forward]
+    return lax.ppermute(block, axis, forward), lax.ppermute(block, axis, backward)
+
+
+def pad_rows(block):
+    return jnp.pad(block, ((0, -block.shape[0] % tile), (0, 0)))
 
 
 def extended(block, sides, width):
@@ -22,13 +424,6 @@
     return block
 
 
-def bucket_of(relative):
-    distance = jnp.abs(relative)
-    far_bucket = 8 + sum(((distance >= threshold).astype(jnp.int32) for threshold in thresholds))
-    near_bucket = jnp.where(distance < 8, distance, far_bucket)
-    return near_bucket + 16 * (relative > 0).astype(jnp.int32)
-
-
 def contract(left_side, right_side, left_axis, right_axis):
     return lax.dot_general(
         left_side,
@@ -63,27 +458,6 @@
         )
         summed = summed + jnp.repeat(block_sums, block_size, axis=0)
     return summed
-
-
-def diagonal_sums(score_grid):
-    row_total, col_total = score_grid.shape
-    wider_grid = jnp.pad(score_grid, ((0, 0), (0, row_total)))
-    flat_grid = jnp.pad(wider_grid.reshape(-1), (0, row_total))
-    skewed = flat_grid.reshape(row_total, col_total + row_total + 1)
-    return jnp.sum(skewed[:, :col_total], axis=0)
-
-
-def head_slice(matrix, head_number, head_dim):
-    return lax.dynamic_slice_in_dim(matrix, head_number * head_dim, head_dim, 1)
-
-
-def merge_heads(per_head):
-    return jnp.transpose(per_head, (1, 0, 2)).reshape(per_head.shape[1], -1)
-
-
-def head_scores(query_part, key_part, bias_column, bucket, allowed):
-    raw_scores = contract(query_part, key_part, 1, 1)
-    return jnp.where(allowed, raw_scores + jnp.take(bias_column, bucket), negative)
 
 
 def per_device(
@@ -154,32 +528,24 @@
     queries = jnp.dot(first_in, query_w, preferred_element_type=jnp.float32).astype(jnp.bfloat16)
     keys_own = jnp.dot(first_in, key_w, preferred_element_type=jnp.float32).astype(jnp.bfloat16)
     values_own = jnp.dot(first_in, value_w, preferred_element_type=jnp.float32).astype(jnp.bfloat16)
-    key_value = extended(jnp.stack([keys_own, values_own]), (("ctx", 1),), row_count)
-    row_segs = id_rim[1, ::2]
-    row_valid = byte_valid[::2]
-    own_segs = row_segs[row_count : 2 * row_count]
-    wide_range = jnp.arange(3 * row_count, dtype=jnp.int32)
-    own_range = jnp.arange(row_count, dtype=jnp.int32)
-    allowed = (own_segs[:, None] == row_segs[None, :]) & row_valid[None, :]
-    bucket = bucket_of(wide_range[None, :] - row_count - own_range[:, None])
-    head_dim = queries.shape[1] // head_count
-    head_range = jnp.arange(head_count, dtype=jnp.int32)
-
-    def forward_head(head_number):
-        query_part = head_slice(queries, head_number, head_dim)
-        key_part = head_slice(key_value[0], head_number, head_dim)
-        value_part = head_slice(key_value[1], head_number, head_dim)
-        bias_column = lax.dynamic_slice_in_dim(rel_bias, head_number, 1, 1)[:, 0]
-        scores = head_scores(query_part, key_part, bias_column, bucket, allowed)
-        row_max = jnp.max(scores, axis=1, keepdims=True)
-        exponent = jnp.exp(scores - row_max)
-        denominator = jnp.sum(exponent, axis=1, keepdims=True)
-        attn_probs = (exponent / denominator).astype(jnp.bfloat16)
-        head_mix = jnp.dot(attn_probs, value_part, preferred_element_type=jnp.float32)
-        return (head_mix, (row_max + jnp.log(denominator))[:, 0])
-
-    head_out, log_norm = lax.map(forward_head, head_range)
-    attended = merge_heads(head_out).astype(jnp.bfloat16)
+    own_kv = pad_rows(jnp.concatenate([keys_own, values_own], axis=1))
+    before_kv, after_kv = neighbours(own_kv, "ctx")
+    row_segs = segments[0, ::2]
+    before_seg, after_seg = neighbours(row_segs, "ctx")
+    segs = jnp.stack(
+        [
+            jnp.where(cycle_place > 0, before_seg, -2),
+            row_segs,
+            jnp.where(cycle_place < cycle_count - 1, after_seg, 1 << 20),
+        ]
+    )
+    segs = jnp.pad(segs, ((0, 0), (0, -row_count % tile)), constant_values=-3)
+    lines = bias_lines(rel_bias)
+    queries = pad_rows(queries)
+    attended_wide, log_norm = attention_forward(
+        segs, queries, before_kv, own_kv, after_kv, lines, row_count
+    )
+    attended = attended_wide[:row_count]
     middle = start_rows + jnp.dot(attended, out_w, preferred_element_type=jnp.float32)
     inverse_two = inverse_rms(middle)
     normed_two = middle * inverse_two
@@ -220,59 +586,21 @@
     d_branch = d_middle.astype(jnp.bfloat16)
     out_grad = contract(attended, d_branch, 0, 0)
     d_attended = contract(d_branch, out_w, 1, 1).astype(jnp.bfloat16)
-    line_onehot = (
-        bucket_of(wide_range - row_count)[:, None]
-        == jnp.arange(bucket_count, dtype=jnp.int32)[None, :]
-    ).astype(jnp.float32)
-
-    def score_grads(head_number):
-        query_part = head_slice(queries, head_number, head_dim)
-        key_part = head_slice(key_value[0], head_number, head_dim)
-        value_part = head_slice(key_value[1], head_number, head_dim)
-        grad_part = head_slice(d_attended, head_number, head_dim)
-        bias_column = lax.dynamic_slice_in_dim(rel_bias, head_number, 1, 1)[:, 0]
-        scores = head_scores(query_part, key_part, bias_column, bucket, allowed)
-        attn_weights = jnp.exp(scores - log_norm[head_number][:, None])
-        d_prob = contract(grad_part, value_part, 1, 1)
-        delta_row = jnp.sum(attn_weights * d_prob, axis=1)
-        d_score = attn_weights * (d_prob - delta_row[:, None])
-        bias_part = jnp.dot(diagonal_sums(d_score), line_onehot, precision=highest)
-        d_score_low = d_score.astype(jnp.bfloat16)
-        d_query = jnp.dot(d_score_low, key_part, preferred_element_type=jnp.float32)
-        return (attn_weights, d_score_low, d_query, delta_row, bias_part, query_part, grad_part)
-
-    def query_head(head_number):
-        attn_weights, d_score_low, d_query, delta_row, bias_part, query_part, grad_part = (
-            score_grads(head_number)
-        )
-        return (d_query, bias_part, delta_row)
-
-    d_query_heads, bias_heads, delta_heads = lax.map(query_head, head_range)
-    query_rim = extended(jnp.stack([queries, d_attended]), (("ctx", 1),), row_count)
-    stat_rim = extended(jnp.stack([log_norm, delta_heads]), (("ctx", 2),), row_count)
-    allowed_back = (row_segs[:, None] == own_segs[None, :]) & row_valid[:, None]
-    bucket_back = bucket_of(own_range[None, :] - wide_range[:, None] + row_count)
-
-    def key_head(head_number):
-        query_part = head_slice(query_rim[0], head_number, head_dim)
-        grad_part = head_slice(query_rim[1], head_number, head_dim)
-        key_part = head_slice(keys_own, head_number, head_dim)
-        value_part = head_slice(values_own, head_number, head_dim)
-        bias_column = lax.dynamic_slice_in_dim(rel_bias, head_number, 1, 1)[:, 0]
-        scores = head_scores(query_part, key_part, bias_column, bucket_back, allowed_back)
-        attn_weights = jnp.exp(scores - stat_rim[0, head_number][:, None])
-        d_prob = contract(grad_part, value_part, 1, 1)
-        d_score = attn_weights * (d_prob - stat_rim[1, head_number][:, None])
-        d_key = contract(d_score.astype(jnp.bfloat16), query_part, 0, 0)
-        d_value = contract(attn_weights.astype(jnp.bfloat16), grad_part, 0, 0)
-        return (d_key, d_value)
-
-    d_key_heads, d_value_heads = lax.map(key_head, head_range)
-    own_grads = jnp.stack([merge_heads(d_key_heads), merge_heads(d_value_heads)])
-    d_queries = merge_heads(d_query_heads).astype(jnp.bfloat16)
-    d_keys = own_grads[0].astype(jnp.bfloat16)
-    d_values = own_grads[1].astype(jnp.bfloat16)
-    bias_grad = jnp.transpose(bias_heads)
+    d_queries, d_before, d_own, d_after, bias_sums = attention_backward(
+        segs, queries, pad_rows(d_attended), attended_wide, before_kv, own_kv, after_kv, lines,
+        log_norm, row_count,
+    )
+    from_after, from_before = (
+        lax.ppermute(d_before, "ctx", [(i + 1, i) for i in range(cycle_count - 1)]),
+        lax.ppermute(d_after, "ctx", [(i, i + 1) for i in range(cycle_count - 1)]),
+    )
+    d_keyval = d_own + from_after.astype(jnp.float32) + from_before.astype(jnp.float32)
+    d_keyval = d_keyval[:row_count].astype(jnp.bfloat16)
+    d_queries = d_queries[:row_count]
+    width = d_queries.shape[1]
+    d_keys = d_keyval[:, :width]
+    d_values = d_keyval[:, width:]
+    bias_grad = bias_collect(bias_sums, bucket_count, head_count)
     q_grad = contract(first_in, d_queries, 0, 0)
     k_grad = contract(first_in, d_keys, 0, 0)
     v_grad = contract(first_in, d_values, 0, 0)

time: 2730 us -> 903 us (0.33)
  matrix products: 1400 us -> 104 us
  local copies, waits for them, and re-layouts: 626 us -> 134 us
  loops' own time: 96.1 us -> 0 us
  waiting for transfers between devices: 330 us -> 390 us
  Pallas kernels: 0 us -> 57.9 us
  other arithmetic: 140 us -> 107 us
    dot_general x86 -> x14, matrix products: 1300 us -> 49.1 us  [contract(): lax.dot_general(left_side, right_side, (((left_axis,), (right_axis,)), ((...]
    slice x40 -> x1, local copies, waits for them, and re-layouts: 166 us -> 0.8 us  [per_device(): row_segs = segments[0, ::2]]
    reshape x24 -> x1, local copies, waits for them, and re-layouts: 156 us -> 0.61 us  [attention_forward(): seg_rows = segs.reshape(3 * tiles, 1, tile)]
    another operation x3 -> x0, loops' own time: 96.1 us -> none  [the longest x1 32.4 us: per_device(): d_query_heads, bias_heads, delta_heads = lax.map(query_head, head_range)]
    pad x24 -> x4, local copies, waits for them, and re-layouts: 81.8 us -> 2.54 us  [the longest x2 1.88 us: pad_rows(): return jnp.pad(block, ((0, -block.shape[0] % tile), (0, 0)))]
    pallas_call x0 -> x2, Pallas kernels: none -> 57.9 us  [the longest x1 39.4 us: attention_backward(): pl.pallas_call(functools.partial(backward_kernel, row_count=row_count), o...]
    dot_general x36 -> x1, matrix products: 48.6 us -> 0.16 us  [bias_collect(): jnp.einsum('chx,cxb->bh', sums[:, :head_count], onehot, precision=lax.Pre...]
    gather x72 -> x2, local copies, waits for them, and re-layouts: 50.9 us -> 5.7 us  [bias_lines(): jnp.take(rel_bias, buckets.reshape(-1), axis=0)]
  transfers between devices with their start and end apart: 26 -> 26, of which waited for: 9 -> 11; matrix products, arithmetic and copies ran while one was open for 55% -> 22% of each run, Pallas kernels for 0% -> 2%
where the time goes in v1:
time: 903 us; the launch traced here: 893 us
  waiting for transfers between devices  390 us (43%)
  local copies, waits for them, and re-layouts  134 us (15%)
  other arithmetic  107 us (12%)
  matrix products  104 us (12%)
  Pallas kernels  57.9 us (6%)
  blocking collectives  54.9 us (6%)
  starting transfers between devices  30.1 us (3%)
  between operations  15.6 us (2%)
    psum x1, waiting for transfers between devices, per_device(): lax.psum(large_sums[0].astype(jnp.bfloat16), ('ctx', 'dp'))  103 us
    dot_general x14, matrix products, contract(): lax.dot_general(left_side, right_side, (((left_axis,), (right_axis,)), ((...  49.1 us
    reduce_scatter x1, waiting for transfers between devices, per_device(): lax.psum_scatter(gate_grad.astype(jnp.bfloat16), 'ws', scatter_dimension=...  46.3 us
    reduce_scatter x1, waiting for transfers between devices, per_device(): lax.psum_scatter(down_grad.astype(jnp.bfloat16), 'ws', scatter_dimension=...  46.2 us
    reduce_scatter x1, waiting for transfers between devices, per_device(): lax.psum_scatter(up_grad.astype(jnp.bfloat16), 'ws', scatter_dimension=0,...  46 us
    psum x1, blocking collectives, per_device(): lax.psum((conv_grad, score_grad, attn_gain_grad, bias_grad, ff_gain_grad)...  42.3 us
    all_gather x1, waiting for transfers between devices, per_device(): lax.all_gather(w_down, 'ws', axis=0, tiled=True)  40.6 us
    pallas_call x1, Pallas kernels, attention_backward(): pl.pallas_call(functools.partial(backward_kernel, row_count=row_count), o...  39.4 us
  transfers between devices with their start and end apart: 26, of which 11 were waited for; matrix products, arithmetic and copies ran while one was open for 22% of the time, Pallas kernels for 2%

profile of v1, /device:TPU:0, one launch (start us, length us, event | category | flops | bytes accessed | tf_op | source)
XLA Modules:
  0.0 893.4 jit_solution(1053633857931375141)
XLA Ops:
  23.2 12.6 %all_gather.31 = bf16[259,768]{1,0:T(8,128)(2,1)S(1)} all-gather(bf16[259,384]{1,0:T(8,128)(2,1)S(1)} %copy-done.31), channel_id=1, replica_groups=mesh['ctx'=8,'dp'=2,'ws'=2] {'ws'}, dimensions={1}, use_global_device_ids=true | all-gather | bytes 596736 | tf_op jit(solution)/shard_map/all_gather | solution.py:494
  67.5 6.2 reshape.492
  78.8 6.7 reduce_sum.235
  128.2 6.7 reduce_sum.239
  164.6 18.5 %attention_forward.1 = (bf16[512,768]{1,0:T(8,128)(2,1)}, f32[4,8,256]{2,1,0:T(8,128)}) custom-call(s32[3,512]{1,0:T(4,128)} %copy-done.36, bf16[512,768]{1,0:T(8,128)(2,1)} %pad.20.q_ref, bf16[512,1536]{1,0:T(8,128)(2,1)} %collective-permute-done.4.before_ref, bf16[512,1536]{1,0:T(8,128)(2,1)} %fusion.13.own_ref, ...), custom_call_target="tpu_custom_call" | custom-call | tf_op jit(solution)/shard_map/attention_forward/pallas_call | solution.py:342
  188.4 5.9 fusion.67
  194.3 10.8 %all-gather.18.cloned.1.call-done = bf16[768,2048]{1,0:T(8,128)(2,1)} async-done(((bf16[384,2048]{1,0:T(8,128)(2,1)}), bf16[768,2048]{1,0:T(8,128)(2,1)}) %all-gather.18.cloned.1.call-update) | async-done | bytes 3145744 | tf_op jit(solution)/shard_map/all_gather | solution.py:500
  211.0 40.6 %all-gather.20.cloned.1.call-done = bf16[2048,768]{1,0:T(8,128)(2,1)} async-done(((bf16[1024,768]{1,0:T(8,128)(2,1)}), bf16[2048,768]{1,0:T(8,128)(2,1)}) %all-gather.20.cloned.1.call-update) | async-done | bytes 3145744 | tf_op jit(solution)/shard_map/all_gather | solution.py:501
  251.6 9.6 %multiply_convert_fusion = (bf16[504,2048]{1,0:T(8,128)(2,1)S(1)}, bf16[504,2048]{1,0:T(8,128)(2,1)S(1)}, bf16[504,2048]{1,0:T(8,128)(2,1)}) fusion(f32[504,2048]{1,0:T(8,128)} %fusion.67, f32[504,2048]{1,0:T(8,128)} %fusion.68, bf16[2048,768]{1,0:T(8,128)(2,1)} %all-gather.20.cloned.1.call-done, bf16[1,504,768]{2,1,0:T(8,128)(2,1)} %param.31), kind=kOutput, calls=%fused_computation.12 | convolution fusion | flops 1612283904 | bytes 18370560 | tf_op jit(solution)/shard_map/dot_general | solution.py:428
  271.2 39.4 %attention_backward.1 = (bf16[512,768]{1,0:T(8,128)(2,1)}, bf16[512,1536]{1,0:T(8,128)(2,1)}, f32[512,1536]{1,0:T(8,128)}, bf16[512,1536]{1,0:T(8,128)(2,1)}, f32[7,16,256]{2,1,0:T(8,128)}) custom-call(s32[3,512]{1,0:T(4,128)} %copy-done.36, bf16[512,768]{1,0:T(8,128)(2,1)} %pad.20.q_ref, bf16[512,768]{1,0:T(8,128)(2,1)} %pad.23.do_ref, ...), custom_call_target="tpu_custom_call" | custom-call | tf_op jit(solution)/shard_map/attention_backward/pallas_call | solution.py:376
  345.8 6.5 broadcast_in_dim.84
  379.6 5.9 reshape.499
  387.4 12.8 %add_reduce_fusion.2 = (f32[504,768]{1,0:T(8,128)}, f32[504,768]{1,0:T(8,128)}) fusion(f32[768]{0:T(1024)S(1)} %copy-done.52, f32[504,2]{1,0:T(8,128)} %mul.515, f32[504,2]{1,0:T(8,128)S(1)} %mul.512, f32[504,768]{1,0:T(8,128)} %copy-done.7, f32[504,2]{1,0:T(8,128)} %mul.529, f32[504,2]{1,0:T(8,128)} %mul.526), kind=kLoop, calls=%fused_computation.38 | loop fusion | flops 5419008 | bytes 4664064 | tf_op jit(solution)/shard_map/reduce_sum | solution.py:456
  425.1 6.7 multiply_reduce_fusion.1
  431.9 6.6 collective-permute-start.8
  481.8 16.5 %reduce-scatter.17.cloned.1.call-done = bf16[384,768]{1,0:T(8,128)(2,1)} async-done(((bf16[768,768]{1,0:T(8,128)(2,1)}), bf16[384,768]{1,0:T(8,128)(2,1)}) %reduce-scatter.17.cloned.1.call-update) | async-done | bytes 589840 | tf_op jit(solution)/shard_map/reduce_scatter | solution.py:668
  498.3 24.5 %reduce-scatter.11.cloned.1.call-done = bf16[384,768]{1,0:T(8,128)(2,1)} async-done(((bf16[768,768]{1,0:T(8,128)(2,1)}), bf16[384,768]{1,0:T(8,128)(2,1)}) %reduce-scatter.11.cloned.1.call-update) | async-done | bytes 589840 | tf_op jit(solution)/shard_map/reduce_scatter | solution.py:659
  522.7 24.7 %reduce-scatter.13.cloned.1.call-done = bf16[384,768]{1,0:T(8,128)(2,1)} async-done(((bf16[768,768]{1,0:T(8,128)(2,1)}), bf16[384,768]{1,0:T(8,128)(2,1)}) %reduce-scatter.13.cloned.1.call-update) | async-done | bytes 589840 | tf_op jit(solution)/shard_map/reduce_scatter | solution.py:662
  547.5 24.4 %reduce-scatter.15.cloned.1.call-done = bf16[384,768]{1,0:T(8,128)(2,1)} async-done(((bf16[768,768]{1,0:T(8,128)(2,1)}), bf16[384,768]{1,0:T(8,128)(2,1)}) %reduce-scatter.15.cloned.1.call-update) | async-done | bytes 589840 | tf_op jit(solution)/shard_map/reduce_scatter | solution.py:665
  571.9 46.3 %reduce-scatter.19.cloned.1.call-done = bf16[384,2048]{1,0:T(8,128)(2,1)} async-done(((bf16[768,2048]{1,0:T(8,128)(2,1)}), bf16[384,2048]{1,0:T(8,128)(2,1)}) %reduce-scatter.19.cloned.1.call-update) | async-done | bytes 1572880 | tf_op jit(solution)/shard_map/reduce_scatter | solution.py:671
  618.2 46.0 %reduce-scatter.21.cloned.1.call-done = bf16[384,2048]{1,0:T(8,128)(2,1)} async-done(((bf16[768,2048]{1,0:T(8,128)(2,1)}), bf16[384,2048]{1,0:T(8,128)(2,1)}) %reduce-scatter.21.cloned.1.call-update) | async-done | bytes 1572880 | tf_op jit(solution)/shard_map/reduce_scatter | solution.py:674
  664.2 46.2 %reduce-scatter.23.cloned.1.call-done = bf16[1024,768]{1,0:T(8,128)(2,1)} async-done(((bf16[2048,768]{1,0:T(8,128)(2,1)}), bf16[1024,768]{1,0:T(8,128)(2,1)}) %reduce-scatter.23.cloned.1.call-update) | async-done | bytes 1572880 | tf_op jit(solution)/shard_map/reduce_scatter | solution.py:677
  725.7 42.3 %all-reduce.5 = (f32[5,768]{1,0:T(8,128)}, f32[768]{0:T(1024)}, f32[768]{0:T(1024)}, f32[32,12]{0,1:T(8,128)}, f32[768]{0:T(1024)}) all-reduce(f32[5,768]{1,0:T(8,128)S(1)} %stack.89, f32[768]{0:T(1024)S(1)} %add_add_fusion.3, f32[768]{0:T(1024)S(1)} %copy-done.65, ...), channel_id=1, replica_groups=mesh['ctx'=8,'dp'=2,'ws'=2] {'ctx','dp','ws'}, use_global_device_ids=true, to_apply=%region_25.26 | all-reduce | flops 6528 | bytes 52224 | tf_op jit(solution)/shard_map/psum | solution.py:691
  770.9 102.9 %all-reduce.9.cloned.1.call-done = (bf16[259,384]{1,0:T(8,128)(2,1)}, bf16[384,768]{1,0:T(8,128)(2,1)}, bf16[384,768]{1,0:T(8,128)(2,1)}, bf16[384,768]{1,0:T(8,...) async-done(((bf16[259,384]{1,0:T(8,128)(2,1)}, bf16[384,768]{1,0:T(8,128)(2,1)}, ...) | async-done | bytes 7276816 | tf_op jit(solution)/shard_map/psum | solution.py:682
  (376 shorter events, 308.4 us)
Async XLA Ops:
  7.2 132.4 %all-gather.12.cloned.1.call-start = ((), (), s32[]{:S(2)}) async-start(), calls=%async_computation.10 | async-start | bytes 1769472 | tf_op jit(solution)/shard_map/all_gather | solution.py:497
  7.9 134.8 %all-gather.10.cloned.1.call-start = ((), (), s32[]{:S(2)}) async-start(), calls=%async_computation.9 | async-start | bytes 1769472 | tf_op jit(solution)/shard_map/all_gather | solution.py:496
  8.7 152.7 %all-gather.8.cloned.1.call-start = ((), (), s32[]{:S(2)}) async-start(), calls=%async_computation.8 | async-start | bytes 1769472 | tf_op jit(solution)/shard_map/all_gather | solution.py:495
  9.5 173.8 %all-gather.14.cloned.1.call-start = ((), (), s32[]{:S(2)}) async-start(), calls=%async_computation.11 | async-start | bytes 1769472 | tf_op jit(solution)/shard_map/all_gather | solution.py:498
  10.0 178.3 %all-gather.16.cloned.1.call-start = ((), (), s32[]{:S(2)}) async-start(), calls=%async_computation.12 | async-start | bytes 4718592 | tf_op jit(solution)/shard_map/all_gather | solution.py:499
  10.6 194.5 %all-gather.18.cloned.1.call-start = ((), (), s32[]{:S(2)}) async-start(), calls=%async_computation.13 | async-start | bytes 4718592 | tf_op jit(solution)/shard_map/all_gather | solution.py:500
  11.2 240.4 %all-gather.20.cloned.1.call-start = ((), (), s32[]{:S(2)}) async-start(), calls=%async_computation.14 | async-start | bytes 4718592 | tf_op jit(solution)/shard_map/all_gather | solution.py:501
  11.3 25.7 %collective-permute-start = (s32[2,1008]{1,0:T(2,128)S(1)}, s32[2,1008]{1,0:T(2,128)S(1)}, u32[]{:S(2)}, u32[]{:S(2)}) collective-permute-start(s32[2,1008]{1,0:T(2,128)S(1)} %pad_add_fusion), channel_id=1, source_target_pairs={{0,4},{4,8},{8,12},{12,16},{16,20},{20,24},{24,28},{1,5},{5,9},{9,... | collective-permute-start | bytes 24200 | tf_op jit(solution)/shard_map/ppermute | solution.py:419
  13.6 23.4 %collective-permute-start.1 = (s32[2,1008]{1,0:T(2,128)S(1)}, s32[2,1008]{1,0:T(2,128)S(1)}, u32[]{:S(2)}, u32[]{:S(2)}) collective-permute-start(s32[2,1008]{1,0:T(2,128)S(1)} %pad_add_fusion), channel_id=1, source_target_pairs={{4,0},{8,4},{12,8},{16,12},{20,16},{24,20},{28,24},{5,1},{9,5},{13... | collective-permute-start | bytes 24200 | tf_op jit(solution)/shard_map/ppermute | solution.py:422
  15.7 143.1 %collective-permute-start.2 = (s32[504]{0:T(512)}, s32[504]{0:T(512)}, u32[]{:S(2)}, u32[]{:S(2)}) collective-permute-start(s32[504]{0:T(512)} %bitcast.13), channel_id=1, source_target_pairs={{0,4},{4,8},{8,12},{12,16},{16,20},{20,24},{24,28},{1,5},{5,9},{9,... | collective-permute-start | bytes 6056 | tf_op jit(solution)/shard_map/ppermute | solution.py:407
  21.5 137.3 %collective-permute-start.3 = (s32[504]{0:T(512)}, s32[504]{0:T(512)}, u32[]{:S(2)}, u32[]{:S(2)}) collective-permute-start(s32[504]{0:T(512)} %bitcast.13), channel_id=1, source_target_pairs={{4,0},{8,4},{12,8},{16,12},{20,16},{24,20},{28,24},{5,1},{9,5},{13... | collective-permute-start | bytes 6056 | tf_op jit(solution)/shard_map/ppermute | solution.py:407
  22.8 457.1 %reduce-scatter.25.cloned.1.call-start = ((), (), s32[]{:S(2)}) async-start(), calls=%async_computation.22 | async-start | bytes 884736
  146.4 18.2 %collective-permute-start.4 = (bf16[512,1536]{1,0:T(8,128)(2,1)}, bf16[512,1536]{1,0:T(8,128)(2,1)}, u32[]{:S(2)}, u32[]{:S(2)}) collective-permute-start(bf16[512,1536]{1,0:T(8,128)(2,1)} %fusion.13.own_ref), channel_id=1, source_target_pairs={{0,4},{4,8},{8,12},{12,16},{16,20},{20,24},{24,28},{1,5},{5,9},{9,... | collective-permute-start | bytes 4718600 | tf_op jit(solution)/shard_map/ppermute | solution.py:407
  150.3 14.3 %collective-permute-start.5 = (bf16[512,1536]{1,0:T(8,128)(2,1)}, bf16[512,1536]{1,0:T(8,128)(2,1)}, u32[]{:S(2)}, u32[]{:S(2)}) collective-permute-start(bf16[512,1536]{1,0:T(8,128)(2,1)} %fusion.13.own_ref), channel_id=1, source_target_pairs={{4,0},{8,4},{12,8},{16,12},{20,16},{24,20},{28,24},{5,1},{9,5},{13... | collective-permute-start | bytes 4718600 | tf_op jit(solution)/shard_map/ppermute | solution.py:407
  310.6 17.3 %collective-permute-start.6 = (bf16[512,1536]{1,0:T(8,128)(2,1)}, bf16[512,1536]{1,0:T(8,128)(2,1)}, u32[]{:S(2)}, u32[]{:S(2)}) collective-permute-start(bf16[512,1536]{1,0:T(8,128)(2,1)} %get-tuple-element.26), channel_id=1, source_target_pairs={{4,0},{8,4},{12,8},{16,12},{20,16},{24,20},{28,24},{5,1},{9,5},{13... | collective-permute-start | bytes 4718600 | tf_op jit(solution)/shard_map/ppermute | solution.py:594
  311.9 16.0 %collective-permute-start.7 = (bf16[512,1536]{1,0:T(8,128)(2,1)}, bf16[512,1536]{1,0:T(8,128)(2,1)}, u32[]{:S(2)}, u32[]{:S(2)}) collective-permute-start(bf16[512,1536]{1,0:T(8,128)(2,1)} %get-tuple-element.27), channel_id=1, source_target_pairs={{0,4},{4,8},{8,12},{12,16},{16,20},{20,24},{24,28},{1,5},{5,9},{9,... | collective-permute-start | bytes 4718600 | tf_op jit(solution)/shard_map/ppermute | solution.py:595
  450.1 48.2 %reduce-scatter.17.cloned.1.call-start = ((), (), s32[]{:S(2)}) async-start(), calls=%async_computation.18 | async-start | bytes 1769472 | tf_op jit(solution)/shard_map/reduce_scatter | solution.py:668
  453.6 69.1 %reduce-scatter.11.cloned.1.call-start = ((), (), s32[]{:S(2)}) async-start(), calls=%async_computation.15 | async-start | bytes 1769472 | tf_op jit(solution)/shard_map/reduce_scatter | solution.py:659
  456.9 90.6 %reduce-scatter.13.cloned.1.call-start = ((), (), s32[]{:S(2)}) async-start(), calls=%async_computation.16 | async-start | bytes 1769472 | tf_op jit(solution)/shard_map/reduce_scatter | solution.py:662
  460.2 111.7 %reduce-scatter.15.cloned.1.call-start = ((), (), s32[]{:S(2)}) async-start(), calls=%async_computation.17 | async-start | bytes 1769472 | tf_op jit(solution)/shard_map/reduce_scatter | solution.py:665
  463.4 154.8 %reduce-scatter.19.cloned.1.call-start = ((), (), s32[]{:S(2)}) async-start(), calls=%async_computation.19 | async-start | bytes 4718592 | tf_op jit(solution)/shard_map/reduce_scatter | solution.py:671
  469.0 195.3 %reduce-scatter.21.cloned.1.call-start = ((), (), s32[]{:S(2)}) async-start(), calls=%async_computation.20 | async-start | bytes 4718592 | tf_op jit(solution)/shard_map/reduce_scatter | solution.py:674
  474.4 236.0 %reduce-scatter.23.cloned.1.call-start = ((), (), s32[]{:S(2)}) async-start(), calls=%async_computation.21 | async-start | bytes 4718592 | tf_op jit(solution)/shard_map/reduce_scatter | solution.py:677
  479.7 394.1 %all-reduce.9.cloned.1.call-start = ((), (), s32[]{:S(2)}) async-start(), calls=%async_computation.23 | async-start | bytes 14561280 | tf_op jit(solution)/shard_map/psum | solution.py:682
  (88 other events, 1016.6 us)
Sparse Core Ops, SparseCore 0:
  9.6 29.8 all-gather.11
  41.0 22.7 all-gather.9
  65.3 22.7 all-gather.7
  89.6 22.7 all-gather.13
  113.8 44.9 all-gather.15
  160.1 44.9 all-gather.17
  206.6 44.9 all-gather.19
  450.2 23.3 reduce-scatter.24
  476.5 21.7 reduce-scatter.16
  500.9 21.7 reduce-scatter.10
  525.6 21.7 reduce-scatter.12
  550.1 21.7 reduce-scatter.14
  574.8 43.3 reduce-scatter.18
  620.9 43.3 reduce-scatter.20
  667.0 43.3 reduce-scatter.22
  715.5 158.2 all-reduce.8
